TPU v7x, 256 devices: a whole 4x4x8 slice. The times are simulated.
256 devices in a mesh: dp: 4 (over x), space: 64 (over y, z, core).
Axes of the slice: x: 4, y: 4, z: 8, core: 2. Of those that a mesh axis runs over, the one named last changes fastest.
Arguments:
- features: bfloat16 [4, 64, 96, 1024], P('dp', 'space'), may hold values from -6 to 6
- cotangent: bfloat16 [4, 64, 192, 128], P('dp', 'space'), may hold values from -6 to 6
- conv_weight: bfloat16 [96, 2592], replicated, may hold values from -0.125 to 0.125
- down_weight: bfloat16 [192, 768], replicated, may hold values from -0.21875 to 0.21875
- neighbours: int32 [4, 64, 26], P('dp', 'space'), may hold values from -1 to 63, as said below
Outputs:
- coarse_out: bfloat16 [4, 64, 192, 128], P('dp', 'space')
- grad_features: float32 [4, 64, 96, 1024], P('dp', 'space')
- grad_conv: float32 [96, 2592], replicated
- grad_down: float32 [192, 768], replicated
Inputs may be any that keep to these rules, and one draw needn't show every extreme that they name: The blocks of a tile sit at distinct cells of a grid; if neighbours[t, s, d] = p is not -1 then neighbours[t, p, 25 - d] = s; a row never names its own block and names a device at most once.
All inputs are finite; a program needn't handle non-finite values.
Results may differ from a plain program's by a relative error of at most 0.0095.
Values may be sent and summed in bfloat16 or wider, within the bound.
No kernel may reach another device: no remote copies, remote signals or barrier semaphores. Data moves between devices by JAX's collectives and lax.ppermute only.
A program may use at most 128 MiB of HBM per device.

v0:
```python
import jax
import jax.numpy as jnp
from jax import lax
from jax.sharding import PartitionSpec as P

BRICK = 8
DIRECTIONS = [
    (step_x, step_y, step_z)
    for step_x in (-1, 0, 1)
    for step_y in (-1, 0, 1)
    for step_z in (-1, 0, 1)
    if (step_x, step_y, step_z) != (0, 0, 0)
]
EPSILON = 1e-06


def cut_inner(offset, extent):
    if offset < 0:
        return slice(0, 1)
    if offset > 0:
        return slice(extent - 1, extent)
    return slice(0, extent)


def cut_outer(offset, extent):
    if offset < 0:
        return slice(0, 1)
    if offset > 0:
        return slice(extent + 1, extent + 2)
    return slice(1, extent + 1)


def inner_layer(block_data, offset):
    return block_data[
        :,
        cut_inner(offset[0], block_data.shape[1]),
        cut_inner(offset[1], block_data.shape[2]),
        cut_inner(offset[2], block_data.shape[3]),
    ]


def outer_layer(padded, offset):
    return padded[
        :,
        cut_outer(offset[0], padded.shape[1] - 2),
        cut_outer(offset[1], padded.shape[2] - 2),
        cut_outer(offset[2], padded.shape[3] - 2),
    ]


def conv_taps(padded, weight_matrix):
    channels = padded.shape[0]
    size_x, size_y, size_z = (padded.shape[1] - 2, padded.shape[2] - 2, padded.shape[3] - 2)
    accumulated = jnp.zeros((weight_matrix.shape[0], size_x * size_y * size_z), jnp.float32)
    for step_x in range(3):
        for step_y in range(3):
            columns = jnp.concatenate(
                [
                    padded[
                        :,
                        step_x : step_x + size_x,
                        step_y : step_y + size_y,
                        step_z : step_z + size_z,
                    ]
                    for step_z in range(3)
                ],
                axis=0,
            ).reshape(3 * channels, size_x * size_y * size_z)
            start_col = (step_x * 3 + step_y) * 3 * channels
            accumulated = accumulated + jnp.dot(
                weight_matrix[:, start_col : start_col + 3 * channels],
                columns,
                preferred_element_type=jnp.float32,
            )
    return accumulated


def weight_taps(padded, grad_out):
    channels = padded.shape[0]
    size_x, size_y, size_z = (padded.shape[1] - 2, padded.shape[2] - 2, padded.shape[3] - 2)
    blocks_out = []
    for step_x in range(3):
        for step_y in range(3):
            columns = jnp.concatenate(
                [
                    padded[
                        :,
                        step_x : step_x + size_x,
                        step_y : step_y + size_y,
                        step_z : step_z + size_z,
                    ]
                    for step_z in range(3)
                ],
                axis=0,
            ).reshape(3 * channels, size_x * size_y * size_z)
            blocks_out.append(
                lax.dot_general(
                    grad_out, columns, (((1,), (1,)), ((), ())), preferred_element_type=jnp.float32
                )
            )
    return jnp.concatenate(blocks_out, axis=1)


def flipped(weight_matrix):
    channels = weight_matrix.shape[0]
    return (
        weight_matrix.reshape(channels, 27, channels)[:, ::-1, :]
        .transpose(2, 1, 0)
        .reshape(channels, 27 * channels)
    )


def coarse_patches(hidden_block):
    channels, size_x, size_y, size_z = hidden_block.shape
    split = hidden_block.reshape(channels, size_x // 2, 2, size_y // 2, 2, size_z // 2, 2)
    return split.transpose(2, 4, 6, 0, 1, 3, 5).reshape(
        8 * channels, size_x // 2 * (size_y // 2) * (size_z // 2)
    )


def from_patches(patch_data, channels, size_x, size_y, size_z):
    split = patch_data.reshape(2, 2, 2, channels, size_x // 2, size_y // 2, size_z // 2)
    return split.transpose(3, 4, 0, 5, 1, 6, 2).reshape(channels, size_x * size_y * size_z)


def silu_slope(activation):
    sigmoid_value = jax.nn.sigmoid(activation)
    return sigmoid_value * (1.0 + activation * (1.0 - sigmoid_value))


def normalized(accumulated):
    return accumulated * lax.rsqrt(jnp.mean(accumulated * accumulated) + EPSILON)


def shards(features, cotangent, conv_weight, down_weight, neighbours):
    channels = features.shape[2]
    block_side = BRICK
    block_depth = features.shape[3] // (block_side * block_side)
    peer_count = lax.axis_size("space")
    capacity = max(block_side * block_side, block_side * block_depth)
    owner_row = neighbours[0, 0]
    present = owner_row >= 0
    target = jnp.where(present, owner_row, peer_count)
    source = jnp.clip(owner_row, 0, peer_count - 1)

    def pack_faces(face_layers, wire_type):
        stacked = jnp.stack(
            [
                jnp.pad(
                    face_layer.reshape(channels, -1), ((0, 0), (0, capacity - face_layer[0].size))
                )
                for face_layer in face_layers
            ]
        )
        return (
            jnp.zeros((peer_count, channels, capacity), wire_type)
            .at[target]
            .set(stacked, mode="drop")
        )

    def unpack_faces(received, shapes):
        picked = jnp.take(received, source, axis=0) * present[:, None, None].astype(received.dtype)
        pieces = []
        for number, shape in enumerate(shapes):
            count = shape[1] * shape[2] * shape[3]
            pieces.append(picked[number, :, :count].reshape(shape))
        return pieces

    def fill_rim(block_data, received):
        padded = jnp.pad(block_data, ((0, 0), (1, 1), (1, 1), (1, 1)))
        pieces = unpack_faces(
            received, [inner_layer(block_data, offset).shape for offset in DIRECTIONS]
        )
        for offset, face_piece in zip(DIRECTIONS, pieces):
            padded = padded.at[
                :,
                cut_outer(offset[0], block_side),
                cut_outer(offset[1], block_side),
                cut_outer(offset[2], block_depth),
            ].set(face_piece)
        return padded

    own_block = features[0, 0].reshape(channels, block_side, block_side, block_depth)
    sent = pack_faces([inner_layer(own_block, offset) for offset in DIRECTIONS], jnp.bfloat16)
    received = lax.all_to_all(sent, "space", split_axis=0, concat_axis=0, tiled=True)
    padded = fill_rim(own_block, received)
    preact = conv_taps(padded, conv_weight)
    hidden = jax.nn.silu(preact).astype(jnp.bfloat16)
    patches = coarse_patches(hidden.reshape(channels, block_side, block_side, block_depth))
    coarse_out = jnp.dot(down_weight, patches, preferred_element_type=jnp.float32).astype(
        jnp.bfloat16
    )
    cot_block = cotangent[0, 0]
    down_part = lax.dot_general(
        cot_block, patches, (((1,), (1,)), ((), ())), preferred_element_type=jnp.float32
    )
    spread_back = from_patches(
        jnp.dot(down_weight.T, cot_block, preferred_element_type=jnp.float32),
        channels,
        block_side,
        block_side,
        block_depth,
    )
    grad_pre = (spread_back * silu_slope(preact)).astype(jnp.bfloat16)
    conv_part = weight_taps(padded, grad_pre)
    flip_weight = flipped(conv_weight)
    grad_block = grad_pre.reshape(channels, block_side, block_side, block_depth)
    widened = jnp.pad(grad_block, ((0, 0), (2, 2), (2, 2), (2, 2)))
    full_grad = conv_taps(widened, flip_weight).reshape(
        channels, block_side + 2, block_side + 2, block_depth + 2
    )
    spill_buffer = pack_faces(
        [outer_layer(full_grad, offset) for offset in DIRECTIONS], jnp.float32
    )
    got_spill = lax.all_to_all(
        spill_buffer.astype(jnp.bfloat16), "space", split_axis=0, concat_axis=0, tiled=True
    ).astype(spill_buffer.dtype)
    inner_part = full_grad[:, 1:-1, 1:-1, 1:-1]
    pieces = unpack_faces(
        got_spill, [inner_layer(inner_part, offset).shape for offset in DIRECTIONS]
    )
    for offset, face_piece in zip(DIRECTIONS, pieces):
        inner_part = inner_part.at[
            :,
            cut_inner(offset[0], block_side),
            cut_inner(offset[1], block_side),
            cut_inner(offset[2], block_depth),
        ].add(face_piece)
    grad_features = inner_part.reshape(channels, -1)
    conv_sum, down_sum = lax.psum((conv_part, down_part), ("dp", "space"))
    return (
        coarse_out[None, None],
        grad_features[None, None],
        normalized(conv_sum),
        normalized(down_sum),
    )


def solution(mesh):
    placed = (
        P("dp", "space", None, None),
        P("dp", "space", None, None),
        P(),
        P(),
        P("dp", "space", None),
    )
    return jax.shard_map(
        shards,
        mesh=mesh,
        in_specs=placed,
        out_specs=(P("dp", "space", None, None), P("dp", "space", None, None), P(), P()),
        check_vma=False,
    )
```

profile of v0, /device:TPU:2, one launch (start us, length us, event | category | flops | bytes accessed | tf_op | source)
XLA Modules:
  0.0 610.5 jit_solution(4286179501511224729)
XLA Ops:
  10.8 5.3 scatter_fusion
  16.1 12.1 %all-to-all-start = ((bf16[64,96,128]{2,1,0:T(8,128)(2,1)}), bf16[64,96,128]{2,1,0:T(8,128)(2,1)S(1)}, u32[]{:S(2)}, u32[]{:S(2)}) async-start(bf16[64,96,128]{2,1,0:T(8,128)(2,1)} %scatter_fusion), calls=%async_computation | async-start | bytes 3145728 | tf_op jit(solution)/shard_map/all_to_all | solution.py:185
  31.8 35.9 %all-to-all-done = bf16[64,96,128]{2,1,0:T(8,128)(2,1)S(1)} async-done(((bf16[64,96,128]{2,1,0:T(8,128)(2,1)}), bf16[64,96,128]{2,1,0:T(8,128)(2,1)S(1)}, u32[]{:S(2)}, u32[]{:S(2)}) %all-to-all-start) | async-done | bytes 1572896 | tf_op jit(solution)/shard_map/all_to_all | solution.py:185
  89.4 2.0 multiply_convert_fusion
  96.3 5.5 pad_slice_fusion.2
  101.9 2.2 pad_slice_fusion.1
  105.8 2.4 pad_maximum_fusion.7
  108.2 1.9 reshape.2479
  110.1 2.4 pad_maximum_fusion.6
  112.5 1.9 reshape.2478
  114.4 2.4 pad_maximum_fusion.5
  116.8 1.9 reshape.2477
  118.7 2.4 pad_maximum_fusion.4
  121.1 1.9 reshape.2476
  123.0 2.4 pad_maximum_fusion.3
  125.4 1.9 reshape.2475
  127.2 2.6 pad_maximum_fusion.2
  129.8 1.9 reshape.2474
  131.7 2.4 pad_maximum_fusion.1
  134.1 1.9 reshape.2473
  135.9 2.4 pad_maximum_fusion
  138.3 1.9 reshape.2470
  140.2 2.1 fusion.13
  153.0 1.6 copy.157
  154.9 3.7 scatter_fusion.1
  160.1 7.0 %all-to-all-start.1 = ((bf16[64,96,128]{2,1,0:T(8,128)(2,1)}), bf16[64,96,128]{2,1,0:T(8,128)(2,1)}, u32[]{:S(2)}, u32[]{:S(2)}) async-start(bf16[64,96,128]{2,1,0:T(8,128)(2,1)} %convert_element_type.100), calls=%async_computation.1 | async-start | bytes 3145728 | tf_op jit(solution)/shard_map/all_to_all | solution.py:215
  175.2 2.0 and_reduce_fusion
  177.2 2.0 slice.2776
  179.3 1.9 copy.225
  181.2 1.8 fusion.2
  183.0 257.4 %all-reduce.49.cloned.1.call-done = (f32[96,2592]{1,0:T(8,128)}, f32[192,768]{1,0:T(8,128)}) async-done(((f32[96,2592]{1,0:T(8,128)}, f32[192,768]{1,0:T(8,128)}), (f32[96,2592]{1,0:T(8,128)}, f32[192,768]{1,0:T(8,128)})) %all-reduce.49.cloned.1.call-update) | async-done | bytes 1585168 | tf_op jit(solution)/shard_map/psum | solution.py:230
  440.5 1.8 multiply_reduce_fusion.1
  443.0 2.1 multiply_reduce_fusion
  445.8 2.0 broadcast_multiply_fusion.1
  448.8 3.5 convert_element_type.101
  452.3 3.6 gather_fusion.1
  455.9 1.5 select_multiply_fusion
  459.5 1.5 fusion.34
  461.0 1.7 slice_bitcast_fusion.3
  462.7 1.6 fusion.46
  469.1 2.6 scatter-add.91
  476.0 2.8 add_select_fusion.1
  478.8 4.6 scatter-add.95
  484.4 2.6 fusion.25
  488.5 2.2 copy.169
  491.7 3.0 scatter-add.101
  499.0 2.8 add_select_fusion
  501.8 4.8 scatter-add.105
  507.5 2.3 copy.175
  509.7 4.2 slice_add_fusion.1
  513.9 18.6 %scatter-add.106 = f32[96,8,8,16]{3,0,2,1:T(8,128)S(1)} dynamic-update-slice(f32[96,8,8,16]{3,0,2,1:T(8,128)S(1)} %scatter-add.105, f32[96,8,8,1]{3,0,2,1:T(8,128)} %slice_add_fusion.1, s32[]{:T(128)} %constant.1634.clone.1, s32[]{:T(128)} %constant.1634.clone.1, s32[]{:T(128)} %constant.1634.clone.1, s32[]{:T(128)} %constant.1634.clone.1) | dynamic-update-slice | bytes 49156 | tf_op jit(solution)/shard_map/scatter-add | solution.py:228
  532.6 2.2 copy.177
  534.9 4.4 slice_add_fusion
  539.3 23.3 %scatter-add.109 = f32[96,8,8,16]{3,0,2,1:T(8,128)S(1)} dynamic-update-slice(f32[96,8,8,16]{3,0,2,1:T(8,128)S(1)} %scatter-add.106, f32[96,8,8,1]{3,0,2,1:T(8,128)} %slice_add_fusion, s32[]{:T(128)} %constant.1634.clone.1, s32[]{:T(128)} %constant.1634.clone.1, s32[]{:T(128)} %constant.1634.clone.1, s32[]{:T(128)} %constant.1644.clone.1) | dynamic-update-slice | bytes 49156 | tf_op jit(solution)/shard_map/scatter-add | solution.py:228
  565.0 3.0 scatter-add.110
  568.0 1.5 copy.180
  570.5 2.2 copy.183
  573.9 3.6 scatter-add.114
  584.5 2.6 scatter-add.120
  587.1 1.5 copy.188
  589.6 2.2 copy.191
  592.9 3.3 scatter-add.124
  599.3 1.8 copy.194
  601.1 2.0 copy.195
  (323 shorter events, 92.7 us)
Async XLA Ops:
  8.3 1.1 copy-start.39
  16.1 12.3 %copy-start.22 = (bf16[192,768]{1,0:T(8,128)(2,1)S(1)}, bf16[192,768]{1,0:T(8,128)(2,1)}, u32[]{:S(2)}) copy-start(bf16[192,768]{1,0:T(8,128)(2,1)} %param.112) | copy-start | bytes 884740
  16.1 12.5 %copy-start.32 = (bf16[1,1,192,128]{3,2,1,0:T(8,128)(2,1)S(1)}, bf16[1,1,192,128]{3,2,1,0:T(8,128)(2,1)}, u32[]{:S(2)}) copy-start(bf16[1,1,192,128]{3,2,1,0:T(8,128)(2,1)} %param.110) | copy-start | bytes 147460
  16.1 51.6 %all-to-all-start = ((bf16[64,96,128]{2,1,0:T(8,128)(2,1)}), bf16[64,96,128]{2,1,0:T(8,128)(2,1)S(1)}, u32[]{:S(2)}, u32[]{:S(2)}) async-start(bf16[64,96,128]{2,1,0:T(8,128)(2,1)} %scatter_fusion), calls=%async_computation | async-start | bytes 3145728 | tf_op jit(solution)/shard_map/all_to_all | solution.py:185
  28.6 1.8 copy-start.19
  75.3 3.2 copy-start
  77.1 3.2 copy-start.2
  78.9 3.2 copy-start.4
  80.7 3.1 copy-start.6
  87.6 1.8 copy-start.30
  140.2 2.1 copy-start.14
  140.2 2.1 copy-start.18
  142.3 1.3 copy-start.13
  143.6 1.3 copy-start.12
  145.0 1.3 copy-start.11
  146.3 1.3 copy-start.10
  147.7 1.3 copy-start.9
  149.0 1.3 copy-start.8
  151.9 1.1 copy-start.17
  160.1 7.1 %copy-start.7 = (bf16[288,8,8,16]{0,3,2,1:T(8,128)(2,1)S(1)}, bf16[288,8,8,16]{0,3,2,1:T(8,128)(2,1)}, u32[]{:S(2)}) copy-start(bf16[288,8,8,16]{0,3,2,1:T(8,128)(2,1)} %copy-done.6) | copy-start | bytes 1769476
  160.1 8.0 %copy-start.31 = (bf16[96,1024]{1,0:T(8,128)(2,1)S(1)}, bf16[96,1024]{1,0:T(8,128)(2,1)}, u32[]{:S(2)}) copy-start(bf16[96,1024]{1,0:T(8,128)(2,1)} %get-tuple-element.737) | copy-start | bytes 589828
  160.1 288.7 %all-to-all-start.1 = ((bf16[64,96,128]{2,1,0:T(8,128)(2,1)}), bf16[64,96,128]{2,1,0:T(8,128)(2,1)}, u32[]{:S(2)}, u32[]{:S(2)}) async-start(bf16[64,96,128]{2,1,0:T(8,128)(2,1)} %convert_element_type.100), calls=%async_computation.1 | async-start | bytes 3145728 | tf_op jit(solution)/shard_map/all_to_all | solution.py:215
  167.1 1.7 copy-start.5
  167.1 2.7 copy-start.3
  167.1 273.4 %all-reduce.49.cloned.1.call-start = ((), (), s32[]{:S(2)}) async-start(), calls=%async_computation.2 | async-start | bytes 3244032 | tf_op jit(solution)/shard_map/psum | solution.py:230
  168.3 1.8 copy-start.1
  168.8 1.6 copy-start.23
  168.8 1.6 copy-start.24
  168.8 1.6 copy-start.25
  168.8 1.6 copy-start.26
  168.8 1.6 copy-start.27
  169.8 0.9 copy-start.28
  169.8 1.0 copy-start.29
  170.1 2.0 copy-start.33
  172.1 2.3 copy-start.36
  172.1 3.1 copy-start.37
  172.1 3.1 copy-start.38
  445.8 2.0 copy-start.16
  457.4 1.1 copy-start.15
  513.9 18.6 %copy-start.35 = (f32[1,96,64]{2,1,0:T(8,128)S(1)}, f32[1,96,64]{2,1,0:T(8,128)}, u32[]{:S(2)}) copy-start(f32[1,96,64]{2,1,0:T(8,128)} %get-tuple-element.662) | copy-start | bytes 73732
  539.3 23.3 %copy-start.34 = (f32[96,8,1,1]{1,0,3,2:T(8,128)S(1)}, f32[96,8,1,1]{1,0,3,2:T(8,128)}, u32[]{:S(2)}) copy-start(f32[96,8,1,1]{1,0,3,2:T(8,128)} %get-tuple-element.653) | copy-start | bytes 9220
  572.7 1.0 copy-start.20
  591.8 1.0 copy-start.21
Sparse Core Ops, SparseCore 0:
  174.0 266.4 all-reduce.48
where the time goes:
time: 620 us; the launch traced here: 610 us
  waiting for transfers between devices  293 us (47%)
  local copies, waits for them, and re-layouts  177 us (29%)
  other arithmetic  73.2 us (12%)
  matrix products  29.7 us (5%)
  starting transfers between devices  19.2 us (3%)
  between operations  17.5 us (3%)
    psum x1, waiting for transfers between devices, shards(): conv_sum, down_sum = lax.psum((conv_part, down_part), ('dp', 'space'))  257 us
    scatter-add x22, local copies, waits for them, and re-layouts, shards(): inner_part = inner_part.at[:, cut_inner(offset[0], block_side), cut_inner...  75.3 us
    all_to_all x1, waiting for transfers between devices, shards(): lax.all_to_all(sent, 'space', split_axis=0, concat_axis=0, tiled=True)  35.9 us
    another operation x33, local copies, waits for them, and re-layouts  26 us
    concatenate x18, other arithmetic, conv_taps(): jnp.concatenate([padded[:, step_x:step_x + size_x, step_y:step_y + size_y...  24 us
    add x19, other arithmetic, shards(): inner_part = inner_part.at[:, cut_inner(offset[0], block_side), cut_inner...  22.2 us
    dot_general x18, matrix products, conv_taps(): jnp.dot(weight_matrix[:, start_col:start_col + 3 * channels], columns, pr...  19.3 us
    reshape x9, local copies, waits for them, and re-layouts, conv_taps(): columns = jnp.concatenate([padded[:, step_x:step_x + size_x, step_y:step_...  15.8 us
  transfers between devices with their start and end apart: 3, of which 2 were waited for; matrix products, arithmetic and copies ran while one was open for 4% of the time, Pallas kernels for 0%

commit v1 on v0

--- a/solution.py
+++ b/solution.py
@@ -227,7 +227,7 @@
             cut_inner(offset[2], block_depth),
         ].add(face_piece)
     grad_features = inner_part.reshape(channels, -1)
-    conv_sum, down_sum = lax.psum((conv_part, down_part), ("dp", "space"))
+    conv_sum, down_sum = lax.psum(lax.psum((conv_part, down_part), "dp"), "space")
     return (
         coarse_out[None, None],
         grad_features[None, None],

time: 620 us -> 590 us (0.952)
  waiting for transfers between devices: 293 us -> 255 us
  local copies, waits for them, and re-layouts: 177 us -> 184 us
    psum x1 -> x2, waiting for transfers between devices: 257 us -> 220 us  [the longest x1 183 us: shards(): lax.psum(lax.psum((conv_part, down_part), 'dp'), 'space')]
    unnamed x141 -> x171, local copies, waits for them, and re-layouts: 14.3 us -> 15.2 us
  transfers between devices with their start and end apart: 3 -> 4, of which waited for: 2 -> 3; matrix products, arithmetic and copies ran while one was open for 4% -> 5% of each run, Pallas kernels for 0% -> 0%
where the time goes in v1:
time: 590 us; the launch traced here: 580 us
  waiting for transfers between devices  255 us (43%)
  local copies, waits for them, and re-layouts  184 us (31%)
  other arithmetic  74.2 us (13%)
  matrix products  30 us (5%)
  starting transfers between devices  19 us (3%)
  between operations  17.6 us (3%)
    psum x1, waiting for transfers between devices, shards(): lax.psum(lax.psum((conv_part, down_part), 'dp'), 'space')  183 us
    scatter-add x22, local copies, waits for them, and re-layouts, shards(): inner_part = inner_part.at[:, cut_inner(offset[0], block_side), cut_inner...  75.3 us
    psum x1, waiting for transfers between devices, shards(): lax.psum((conv_part, down_part), 'dp')  37.4 us
    all_to_all x1, waiting for transfers between devices, shards(): lax.all_to_all(sent, 'space', split_axis=0, concat_axis=0, tiled=True)  35.3 us
    another operation x33, local copies, waits for them, and re-layouts  26.1 us
    concatenate x18, other arithmetic, conv_taps(): jnp.concatenate([padded[:, step_x:step_x + size_x, step_y:step_y + size_y...  24 us
    add x19, other arithmetic, shards(): inner_part = inner_part.at[:, cut_inner(offset[0], block_side), cut_inner...  22.2 us
    dot_general x18, matrix products, conv_taps(): jnp.dot(weight_matrix[:, start_col:start_col + 3 * channels], columns, pr...  18.9 us
  transfers between devices with their start and end apart: 4, of which 3 were waited for; matrix products, arithmetic and copies ran while one was open for 5% of the time, Pallas kernels for 0%

profile of v1, /device:TPU:2, one launch (start us, length us, event | category | flops | bytes accessed | tf_op | source)
XLA Modules:
  0.0 580.2 jit_solution(2611429841952977329)
XLA Ops:
  10.8 5.3 scatter_fusion
  16.1 12.1 %all-to-all-start = ((bf16[64,96,128]{2,1,0:T(8,128)(2,1)}), bf16[64,96,128]{2,1,0:T(8,128)(2,1)S(1)}, u32[]{:S(2)}, u32[]{:S(2)}) async-start(bf16[64,96,128]{2,1,0:T(8,128)(2,1)} %scatter_fusion), calls=%async_computation | async-start | bytes 3145728 | tf_op jit(solution)/shard_map/all_to_all | solution.py:185
  32.4 35.3 %all-to-all-done = bf16[64,96,128]{2,1,0:T(8,128)(2,1)S(1)} async-done(((bf16[64,96,128]{2,1,0:T(8,128)(2,1)}), bf16[64,96,128]{2,1,0:T(8,128)(2,1)S(1)}, u32[]{:S(2)}, u32[]{:S(2)}) %all-to-all-start) | async-done | bytes 1572896 | tf_op jit(solution)/shard_map/all_to_all | solution.py:185
  88.9 2.0 multiply_convert_fusion
  99.0 5.5 pad_slice_fusion.2
  104.6 2.2 pad_slice_fusion.1
  108.5 2.4 pad_maximum_fusion.7
  110.9 1.9 reshape.2479
  112.8 2.4 pad_maximum_fusion.6
  115.2 1.9 reshape.2478
  117.1 2.4 pad_maximum_fusion.5
  119.5 1.9 reshape.2477
  121.4 2.4 pad_maximum_fusion.4
  123.8 1.9 reshape.2476
  125.7 2.4 pad_maximum_fusion.3
  128.1 1.9 reshape.2475
  130.0 2.6 pad_maximum_fusion.2
  132.6 1.9 reshape.2474
  134.4 2.4 pad_maximum_fusion.1
  136.8 1.9 reshape.2473
  138.7 2.4 pad_maximum_fusion
  141.1 1.9 reshape.2470
  143.0 2.1 fusion.13
  161.5 2.3 concatenate.266
  165.3 1.5 copy.157
  167.5 3.9 scatter_fusion.1
  172.8 6.8 %all-to-all-start.1 = ((bf16[64,96,128]{2,1,0:T(8,128)(2,1)}), bf16[64,96,128]{2,1,0:T(8,128)(2,1)}, u32[]{:S(2)}, u32[]{:S(2)}) async-start(bf16[64,96,128]{2,1,0:T(8,128)(2,1)} %convert_element_type.100), calls=%async_computation.1 | async-start | bytes 3145728 | tf_op jit(solution)/shard_map/all_to_all | solution.py:215
  179.7 37.4 %all-reduce.53.cloned.1.call-done = (f32[96,2592]{1,0:T(8,128)}, f32[192,768]{1,0:T(8,128)}) async-done(((f32[96,2592]{1,0:T(8,128)}, f32[192,768]{1,0:T(8,128)}), (f32[96,2592]{1,0:T(8,128)}, f32[192,768]{1,0:T(8,128)})) %all-reduce.53.cloned.1.call-update) | async-done | bytes 1585168 | tf_op jit(solution)/shard_map/psum | solution.py:230
  219.2 2.1 and_reduce_fusion
  221.3 2.0 slice.2776
  223.3 1.9 copy.225
  225.3 1.8 fusion.2
  227.1 182.6 %all-reduce.51.cloned.1.call-done = (f32[96,2592]{1,0:T(8,128)}, f32[192,768]{1,0:T(8,128)}) async-done(((f32[96,2592]{1,0:T(8,128)}, f32[192,768]{1,0:T(8,128)}), (f32[96,2592]{1,0:T(8,128)}, f32[192,768]{1,0:T(8,128)})) %all-reduce.51.cloned.1.call-update) | async-done | bytes 1585168 | tf_op jit(solution)/shard_map/psum | solution.py:230
  409.7 1.8 multiply_reduce_fusion.1
  412.2 2.1 multiply_reduce_fusion
  415.0 2.0 broadcast_multiply_fusion.1
  418.1 3.5 convert_element_type.101
  421.6 3.7 gather_fusion.1
  430.5 1.7 slice_bitcast_fusion.3
  432.2 1.5 fusion.46
  438.6 2.6 scatter-add.91
  445.5 2.9 add_select_fusion.1
  448.4 4.7 scatter-add.95
  454.1 2.8 fusion.25
  458.1 2.2 copy.169
  461.3 3.2 scatter-add.101
  468.9 2.9 add_select_fusion
  471.7 4.9 scatter-add.105
  477.5 2.2 copy.175
  479.8 4.2 slice_add_fusion.1
  483.9 18.6 %scatter-add.106 = f32[96,8,8,16]{3,0,2,1:T(8,128)S(1)} dynamic-update-slice(f32[96,8,8,16]{3,0,2,1:T(8,128)S(1)} %scatter-add.105, f32[96,8,8,1]{3,0,2,1:T(8,128)} %slice_add_fusion.1, s32[]{:T(128)} %constant.1634.clone.1, s32[]{:T(128)} %constant.1634.clone.1, s32[]{:T(128)} %constant.1634.clone.1, s32[]{:T(128)} %constant.1634.clone.1) | dynamic-update-slice | bytes 49156 | tf_op jit(solution)/shard_map/scatter-add | solution.py:228
  502.6 2.3 copy.177
  504.9 4.5 slice_add_fusion
  509.4 23.3 %scatter-add.109 = f32[96,8,8,16]{3,0,2,1:T(8,128)S(1)} dynamic-update-slice(f32[96,8,8,16]{3,0,2,1:T(8,128)S(1)} %scatter-add.106, f32[96,8,8,1]{3,0,2,1:T(8,128)} %slice_add_fusion, s32[]{:T(128)} %constant.1634.clone.1, s32[]{:T(128)} %constant.1634.clone.1, s32[]{:T(128)} %constant.1634.clone.1, s32[]{:T(128)} %constant.1644.clone.1) | dynamic-update-slice | bytes 49156 | tf_op jit(solution)/shard_map/scatter-add | solution.py:228
  535.1 3.0 scatter-add.110
  538.1 1.5 copy.180
  540.6 2.2 copy.183
  543.9 3.6 scatter-add.114
  554.3 2.6 scatter-add.120
  556.8 1.5 copy.188
  559.4 2.2 copy.191
  562.7 3.3 scatter-add.124
  569.1 1.8 copy.194
  570.9 2.0 copy.195
  (356 shorter events, 100.0 us)
Async XLA Ops:
  8.3 1.1 copy-start.54
  9.4 6.7 %copy-start.40 = (s32[26]{0:T(128)}, s32[26]{0:T(128)S(1)}, u32[]{:S(2)}) copy-start(s32[26]{0:T(128)S(1)} %get-tuple-element.800) | copy-start | bytes 316
  16.1 12.3 %copy-start.14 = (bf16[192,768]{1,0:T(8,128)(2,1)S(1)}, bf16[192,768]{1,0:T(8,128)(2,1)}, u32[]{:S(2)}) copy-start(bf16[192,768]{1,0:T(8,128)(2,1)} %param.112) | copy-start | bytes 884740
  16.1 12.5 %copy-start.20 = (bf16[1,1,192,128]{3,2,1,0:T(8,128)(2,1)S(1)}, bf16[1,1,192,128]{3,2,1,0:T(8,128)(2,1)}, u32[]{:S(2)}) copy-start(bf16[1,1,192,128]{3,2,1,0:T(8,128)(2,1)} %param.110) | copy-start | bytes 147460
  16.1 51.6 %all-to-all-start = ((bf16[64,96,128]{2,1,0:T(8,128)(2,1)}), bf16[64,96,128]{2,1,0:T(8,128)(2,1)S(1)}, u32[]{:S(2)}, u32[]{:S(2)}) async-start(bf16[64,96,128]{2,1,0:T(8,128)(2,1)} %scatter_fusion), calls=%async_computation | async-start | bytes 3145728 | tf_op jit(solution)/shard_map/all_to_all | solution.py:185
  28.2 188.9 %all-reduce.53.cloned.1.call-start = ((), (), s32[]{:S(2)}) async-start(), calls=%async_computation.3 | async-start | bytes 3244032 | tf_op jit(solution)/shard_map/psum | solution.py:230
  28.6 1.8 copy-start.11
  31.8 36.9 %copy-start.37 = (s32[1024]{0:T(1024)}, s32[1024]{0:T(1024)S(1)}, u32[]{:S(2)}) copy-start(s32[1024]{0:T(1024)S(1)} %pad_clamp_fusion) | copy-start | bytes 12292
  31.9 36.9 %copy-start.38 = (pred[26]{0:T(512)(128)(4,1)}, pred[26]{0:T(512)(128)(4,1)S(1)}, u32[]{:S(2)}) copy-start(pred[26]{0:T(512)(128)(4,1)S(1)} %compare_and_fusion) | copy-start | bytes 82
  87.1 1.8 copy-start.16
  143.0 2.1 copy-start.6
  143.0 2.1 copy-start.10
  145.1 1.3 copy-start.5
  146.4 1.3 copy-start.4
  147.8 1.3 copy-start.3
  149.1 1.3 copy-start.2
  150.5 1.3 copy-start.1
  151.8 1.3 copy-start
  154.6 4.5 copy-start.19
  154.6 5.2 copy-start.21
  154.7 9.1 %copy-start.9 = (f32[96,10,10,18]{0,3,2,1:T(8,128)}, f32[96,10,10,18]{0,3,2,1:T(8,128)S(1)}, u32[]{:S(2)}) copy-start(f32[96,10,10,18]{0,3,2,1:T(8,128)S(1)} %reshape.2481) | copy-start | bytes 2073604
  154.7 6.8 %copy-start.15 = (f32[96,288]{1,0:T(8,128)S(1)}, f32[96,288]{1,0:T(8,128)}, u32[]{:S(2)}) copy-start(f32[96,288]{1,0:T(8,128)} %fusion.71) | copy-start | bytes 331780
  163.8 0.9 copy-start.49
  163.8 1.0 copy-start.36
  163.8 1.0 copy-start.18
  163.8 1.0 copy-start.35
  163.8 1.0 copy-start.48
  163.8 1.0 copy-start.28
  163.8 1.0 copy-start.47
  163.8 1.0 copy-start.34
  163.8 1.1 copy-start.17
  163.9 1.1 copy-start.33
  163.9 1.1 copy-start.25
  163.9 1.1 copy-start.24
  163.9 1.1 copy-start.32
  163.9 1.1 copy-start.31
  163.9 1.2 copy-start.46
  163.9 1.2 copy-start.27
  163.9 1.2 copy-start.45
  163.9 1.2 copy-start.30
  163.9 1.2 copy-start.29
  164.0 1.2 copy-start.44
  164.0 1.3 copy-start.26
  164.0 1.3 copy-start.43
  166.8 0.7 copy-start.41
  172.8 45.6 %copy-start.51 = (s32[4]{0:T(128)S(1)}, s32[4]{0:T(128)}, u32[]{:S(2)}) copy-start(s32[4]{0:T(128)} %constant.1649.clone.1) | copy-start | bytes 52
  172.8 46.3 %copy-start.52 = (s32[4]{0:T(128)S(1)}, s32[4]{0:T(128)}, u32[]{:S(2)}) copy-start(s32[4]{0:T(128)} %constant.1646.clone.1) | copy-start | bytes 52
  172.8 46.3 %copy-start.53 = (s32[4]{0:T(128)S(1)}, s32[4]{0:T(128)}, u32[]{:S(2)}) copy-start(s32[4]{0:T(128)} %constant.1650.clone.1) | copy-start | bytes 52
  172.8 245.2 %all-to-all-start.1 = ((bf16[64,96,128]{2,1,0:T(8,128)(2,1)}), bf16[64,96,128]{2,1,0:T(8,128)(2,1)}, u32[]{:S(2)}, u32[]{:S(2)}) async-start(bf16[64,96,128]{2,1,0:T(8,128)(2,1)} %convert_element_type.100), calls=%async_computation.1 | async-start | bytes 3145728 | tf_op jit(solution)/shard_map/all_to_all | solution.py:215
  179.6 43.6 %copy-start.42 = (f32[96,1,1,1]{0,3,2,1:T(1,128)S(1)}, f32[96,1,1,1]{0,3,2,1:T(1,128)}, u32[]{:S(2)}) copy-start(f32[96,1,1,1]{0,3,2,1:T(1,128)} %get-tuple-element.667) | copy-start | bytes 1156
  179.6 230.1 %all-reduce.51.cloned.1.call-start = ((), (), s32[]{:S(2)}) async-start(), calls=%async_computation.2 | async-start | bytes 3244032 | tf_op jit(solution)/shard_map/psum | solution.py:230
  415.0 2.0 copy-start.8
  421.6 3.7 copy-start.39
  421.6 3.7 copy-start.50
  426.8 1.1 copy-start.7
  483.9 18.6 %copy-start.23 = (f32[1,96,64]{2,1,0:T(8,128)S(1)}, f32[1,96,64]{2,1,0:T(8,128)}, u32[]{:S(2)}) copy-start(f32[1,96,64]{2,1,0:T(8,128)} %get-tuple-element.664) | copy-start | bytes 73732
  509.4 23.3 %copy-start.22 = (f32[96,8,1,1]{1,0,3,2:T(8,128)S(1)}, f32[96,8,1,1]{1,0,3,2:T(8,128)}, u32[]{:S(2)}) copy-start(f32[96,8,1,1]{1,0,3,2:T(8,128)} %get-tuple-element.655) | copy-start | bytes 9220
  542.8 1.0 copy-start.12
  561.5 1.0 copy-start.13
Sparse Core Ops, SparseCore 0:
  164.1 52.8 all-reduce.52
  221.0 188.6 all-reduce.50
